TPU v7x, 256 devices: a whole 4x4x8 slice. The times are simulated.
256 devices in a mesh: seq: 32 (over y_hi, z, core), head: 8 (over x, y_lo).
Axes of the slice: x: 4, y: 4 (y_hi: 2, y_lo: 2; y = y_hi * 2 + y_lo), z: 8, core: 2. Of those that a mesh axis runs over, the one named last changes fastest.
Arguments:
- resid: bfloat16 [8192, 8192], P('seq'), may hold values from -6 to 6
- norm_gain: float32 [8192], replicated, may hold values from 0.1 to 1.9
- sender_diff: bfloat16 [8192, 4096], P('seq', 'head'), may hold values from -6 to 6
- w_out1: bfloat16 [4096, 8192], P('head', 'seq'), may hold values from -0.09375 to 0.09375
- w_query: bfloat16 [8192, 4096], P('seq', 'head')
- w_key: bfloat16 [8192, 1024], P('seq', 'head')
- w_value: bfloat16 [8192, 1024], P('seq', 'head'), may hold values from -0.0625 to 0.0625
- edge_mask: int32 [32, 32], replicated, may hold values 0 or 1
- doc_ids: int32 [32, 256], P('seq'), may hold values from 0 to 3, never falling along the last dimension, each value on 1 to 128 neighbouring positions
Outputs:
- patched: bfloat16 [8192, 4096], P('seq', 'head')
All inputs are finite; a program needn't handle non-finite values.
Results may differ from a plain program's by a relative error of at most 0.0085.
The roundings to bfloat16 on the way count: a program that leaves them out, or rounds other values in their place, can miss the bound.
Values may be sent and summed in bfloat16 or wider, within the bound.
A program may use at most 128 MiB of HBM per device.

v0:
```python
import jax
import jax.numpy as jnp
from jax import lax
from jax.sharding import PartitionSpec as P

HEAD_SIZE = 128
epsilon = 1e-05


def attend(query, keys, values, doc_row, head_dim):
    tokens = query.shape[0]
    groups = keys.shape[1] // head_dim
    query_head_rows = query.reshape(tokens, groups, -1, head_dim)
    key_head_rows = keys.reshape(tokens, groups, head_dim)
    value_head_rows = values.reshape(tokens, groups, head_dim)
    attention_scores = jnp.einsum(
        "pehm,qem->ehpq", query_head_rows, key_head_rows, preferred_element_type=jnp.float32
    ) * head_dim ** (-0.5)
    position = jnp.arange(tokens, dtype=jnp.int32)
    allowed = (doc_row[:, None] == doc_row[None, :]) & (position[None, :] <= position[:, None])
    attention_scores = jnp.where(allowed, attention_scores, -jnp.inf)
    top = jnp.max(attention_scores, axis=-1, keepdims=True)
    attention_weights = jnp.exp(attention_scores - top)
    attention_weights = (
        attention_weights / jnp.sum(attention_weights, axis=-1, keepdims=True)
    ).astype(jnp.bfloat16)
    mixed_values = jnp.einsum(
        "uczp,puv->zucv", attention_weights, value_head_rows, preferred_element_type=jnp.float32
    )
    return mixed_values.astype(jnp.bfloat16).reshape(tokens, -1)


def local(resid, norm_gain, sender_diff, w_out1, w_query, w_key, w_value, edge_mask, doc_ids):
    head_dim = HEAD_SIZE
    query_cols = w_query.shape[1]
    resid_wide = resid.astype(jnp.float32)
    inv_rms = lax.rsqrt(jnp.mean(resid_wide * resid_wide, axis=1) + epsilon)
    normed = (resid_wide * inv_rms[:, None] * norm_gain[None, :]).astype(jnp.bfloat16)
    seq_index = lax.axis_index("seq")
    head_index = lax.axis_index("head")
    receivers = query_cols // head_dim
    senders = edge_mask.shape[0]
    local_mask = lax.dynamic_slice_in_dim(edge_mask, head_index * receivers, receivers, 1).astype(
        jnp.float32
    )
    clean_query = jnp.dot(
        normed,
        lax.all_gather(w_query, "seq", axis=0, tiled=True),
        preferred_element_type=jnp.float32,
    )
    keys = jnp.dot(
        normed, lax.all_gather(w_key, "seq", axis=0, tiled=True), preferred_element_type=jnp.float32
    ).astype(jnp.bfloat16)
    values = jnp.dot(
        normed,
        lax.all_gather(w_value, "seq", axis=0, tiled=True),
        preferred_element_type=jnp.float32,
    ).astype(jnp.bfloat16)
    sender_all = lax.all_gather(sender_diff, "head", axis=1, tiled=True)
    rows_dev = w_query.shape[0]
    gain_rows = lax.dynamic_slice_in_dim(norm_gain, seq_index * rows_dev, rows_dev)
    scaled = (w_query.astype(jnp.float32) * gain_rows[:, None]).astype(jnp.bfloat16)
    partial_virtual = jnp.dot(
        lax.all_gather(w_out1, "head", axis=0, tiled=True),
        scaled,
        preferred_element_type=jnp.float32,
    )
    partial_virtual = (
        partial_virtual.reshape(senders, head_dim, receivers, head_dim)
        * local_mask[:, None, :, None]
    ).reshape(senders * head_dim, query_cols)
    virtual = lax.psum(partial_virtual, "seq").astype(jnp.bfloat16)
    delta = jnp.dot(sender_all, virtual, preferred_element_type=jnp.float32)
    query = (clean_query + inv_rms[:, None] * delta).astype(jnp.bfloat16)
    return attend(query, keys, values, doc_ids[0], head_dim)


def solution(mesh):
    placed = (
        P("seq", None),
        P(),
        P("seq", "head"),
        P("head", "seq"),
        P("seq", "head"),
        P("seq", "head"),
        P("seq", "head"),
        P(),
        P("seq", None),
    )
    return jax.shard_map(
        local, mesh=mesh, in_specs=placed, out_specs=P("seq", "head"), check_vma=False
    )
```

profile of v0, /device:TPU:1, one launch (start us, length us, event | category | flops | bytes accessed | tf_op | source)
XLA Modules:
  0.0 447.9 jit_solution(1219935657815322950)
XLA Ops:
  6.5 0.0 copy-start
  6.5 0.0 all-gather.12.cloned.1.call-start
  6.5 0.7 all-gather.12.cloned.1.call-update
  7.3 0.0 all-gather.10.cloned.1.call-start
  7.3 0.7 all-gather.10.cloned.1.call-update
  8.0 0.0 all-gather.14.cloned.1.call-start
  8.1 0.7 all-gather.14.cloned.1.call-update
  8.7 0.0 all-gather.8.cloned.1.call-start
  8.8 0.5 all-gather.8.cloned.1.call-update
  9.3 0.0 all-gather.6.cloned.1.call-start
  9.4 0.5 all-gather.6.cloned.1.call-update
  9.9 0.0 copy-done
  9.9 0.1 constant_dynamic-slice_fusion
  10.0 0.1 copy.22
  10.1 3.1 fusion
  13.2 0.0 copy-done.3
  13.2 0.1 fusion.30
  13.3 0.1 dynamic_slice.6
  13.4 52.5 %all-gather.12.cloned.1.call-done = bf16[4096,256]{1,0:T(8,128)(2,1)} async-done(((bf16[512,256]{1,0:T(8,128)(2,1)}), bf16[4096,256]{1,0:T(8,128)(2,1)}) %all-gather.12.cloned.1.call-update) | async-done | bytes 2097168 | tf_op jit(solution)/shard_map/all_gather | solution.py:64
  65.9 1.1 mul.77
  67.1 0.4 copy-done.1
  67.5 9.2 %bitcast_multiply_fusion = f32[4096,512]{0,1:T(8,128)} fusion(f32[64,8,32,128]{3,2,1,0:T(8,128)S(1)} %bitcast.54, bf16[4096,256]{1,0:T(8,128)(2,1)S(1)} %copy-done.1, bf16[256,512]{1,0:T(8,128)(2,1)S(1)} %copy-done.2, f32[256]{0:T(256)S(1)} %dynamic_slice.6), kind=kOutput, calls=%fused_computation.5 | convolution fusion | flops 1076232192 | bytes 19137536 | tf_op jit(solution)/shard_map/dot_general | solution.py:63
  76.7 179.3 %all-reduce.1 = bf16[4096,512]{0,1:T(8,128)(2,1)} all-reduce(f32[4096,512]{0,1:T(8,128)} %bitcast_multiply_fusion), channel_id=1, replica_groups=mesh['seq'=32,'head'=8] {'seq'}, use_global_device_ids=true, to_apply=%region_1.0 | all-reduce | flops 2097152 | bytes 12582912 | tf_op jit(solution)/shard_map/psum | solution.py:72
  256.0 7.0 %fusion.31 = f32[256,512]{1,0:T(8,128)S(1)} fusion(bf16[8192,512]{1,0:T(8,128)(2,1)} %all-gather.10.cloned.1.call-done, bf16[256,8192]{1,0:T(8,128)(2,1)} %param.9, f32[8192]{0:T(1024)S(1)} %copy-done.4, f32[256]{0:T(256)S(1)} %add_rsqrt_fusion), kind=kOutput, calls=%fused_computation.34 | convolution fusion | flops 2155872256 | bytes 13140992 | tf_op jit(solution)/shard_map/dot_general | solution.py:46
  263.0 13.7 %all-gather.14.cloned.1.call-done = bf16[256,4096]{1,0:T(8,128)(2,1)} async-done(((bf16[256,512]{1,0:T(8,128)(2,1)}), bf16[256,4096]{1,0:T(8,128)(2,1)}) %all-gather.14.cloned.1.call-update) | async-done | bytes 2097168 | tf_op jit(solution)/shard_map/all_gather | solution.py:59
  276.7 4.2 fusion.19
  280.9 75.8 %all-gather.8.cloned.1.call-done = bf16[8192,128]{1,0:T(8,128)(2,1)} async-done(((bf16[256,128]{1,0:T(8,128)(2,1)}), bf16[8192,128]{1,0:T(8,128)(2,1)}) %all-gather.8.cloned.1.call-update) | async-done | bytes 2097168 | tf_op jit(solution)/shard_map/all_gather | solution.py:52
  356.7 4.5 %fusion.37 = (f32[4,256]{1,0:T(4,128)S(1)}, f32[1,4,256,256]{2,3,1,0:T(8,128)S(1)}) fusion(bf16[32,4,8,128]{3,2,1,0:T(8,128)(2,1)S(1)} %fusion.19, bf16[8192,128]{1,0:T(8,128)(2,1)} %all-gather.8.cloned.1.call-done, bf16[256,8192]{1,0:T(8,128)(2,1)} %param.9, f32[8192]{0:T(1024)S(1)} %copy-done.4, f32[256]{0:T(256)S(1)} %add_rsqrt_fusion, ...), kind=kOutput, calls=%fused_computation.35 | convolution fusion | flops 613186560 | bytes 7705600 | tf_op jit(solution)/shard_map/pehm,qem->ehpq/dot_general | solution.py:16
  361.2 0.2 fusion.24
  361.3 74.5 %all-gather.6.cloned.1.call-done = bf16[8192,128]{1,0:T(8,128)(2,1)} async-done(((bf16[256,128]{1,0:T(8,128)(2,1)}), bf16[8192,128]{1,0:T(8,128)(2,1)}) %all-gather.6.cloned.1.call-update) | async-done | bytes 2097168 | tf_op jit(solution)/shard_map/all_gather | solution.py:56
  435.9 4.7 %convolution_convert_fusion = bf16[128,4,256]{2,0,1:T(8,128)(2,1)S(1)} fusion(bf16[8192,128]{1,0:T(8,128)(2,1)} %all-gather.6.cloned.1.call-done, f32[1,4,256,256]{2,3,1,0:T(8,128)S(1)} %get-tuple-element.6, f32[4,256]{1,0:T(4,128)S(1)} %fusion.24, f32[4,256]{1,0:T(4,128)S(1)} %get-tuple-element.5, bf16[256,8192]{1,0:T(8,128)(2,1)} %param.9, ...), kind=kOutput, calls=%fused_computation.14 | convolution fusion | flops 613318656 | bytes 7644160 | tf_op jit(solution)/shard_map/uczp,puv->zucv/dot_general | solution.py:27
  440.5 0.8 copy.19
  (9 shorter events, 0.0 us)
Async XLA Ops:
  6.5 3.4 copy-start
  6.5 6.7 %copy-start.3 = (s32[1,256]{1,0:T(1,128)S(1)}, s32[1,256]{1,0:T(1,128)}, u32[]{:S(2)}) copy-start(s32[1,256]{1,0:T(1,128)} %param.17) | copy-start | bytes 3076
  6.5 6.8 %copy-start.4 = (f32[8192]{0:T(1024)S(1)}, f32[8192]{0:T(1024)}, u32[]{:S(2)}) copy-start(f32[8192]{0:T(1024)} %param.10) | copy-start | bytes 98308
  6.5 59.4 %all-gather.12.cloned.1.call-start = ((), (), s32[]{:S(2)}) async-start(), calls=%async_computation.3 | async-start | bytes 2359296 | tf_op jit(solution)/shard_map/all_gather | solution.py:64
  7.3 248.7 %all-gather.10.cloned.1.call-start = ((), (), s32[]{:S(2)}) async-start(), calls=%async_computation.2 | async-start | bytes 8650752 | tf_op jit(solution)/shard_map/all_gather | solution.py:48
  8.0 268.7 %all-gather.14.cloned.1.call-start = ((), (), s32[]{:S(2)}) async-start(), calls=%async_computation.4 | async-start | bytes 2359296 | tf_op jit(solution)/shard_map/all_gather | solution.py:59
  8.7 347.9 %all-gather.8.cloned.1.call-start = ((), (), s32[]{:S(2)}) async-start(), calls=%async_computation.1 | async-start | bytes 2162688 | tf_op jit(solution)/shard_map/all_gather | solution.py:52
  9.3 426.5 %all-gather.6.cloned.1.call-start = ((), (), s32[]{:S(2)}) async-start(), calls=%async_computation | async-start | bytes 2162688 | tf_op jit(solution)/shard_map/all_gather | solution.py:56
  13.4 53.6 %copy-start.2 = (bf16[256,512]{1,0:T(8,128)(2,1)S(1)}, bf16[256,512]{1,0:T(8,128)(2,1)}, u32[]{:S(2)}) copy-start(bf16[256,512]{1,0:T(8,128)(2,1)} %param.13) | copy-start | bytes 786436
  65.9 1.6 copy-start.1
Sparse Core Ops, SparseCore 0:
  9.2 56.7 all-gather.11
  68.7 133.9 all-gather.9
  204.5 72.1 all-gather.13
  279.3 77.2 all-gather.7
  359.3 76.5 all-gather.5
where the time goes:
time: 448 us
  waiting for transfers between devices  220 us (49%)
  blocking collectives  179 us (40%)
  matrix products  29.5 us (7%)
  between operations  13.2 us (3%)
    psum x1, blocking collectives, local(): virtual = lax.psum(partial_virtual, 'seq').astype(jnp.bfloat16)  179 us
    all_gather x1, waiting for transfers between devices, local(): lax.all_gather(w_key, 'seq', axis=0, tiled=True)  75.8 us
    all_gather x1, waiting for transfers between devices, local(): lax.all_gather(w_value, 'seq', axis=0, tiled=True)  74.5 us
    all_gather x1, waiting for transfers between devices, local(): lax.all_gather(w_out1, 'head', axis=0, tiled=True)  52.5 us
    all_gather x1, waiting for transfers between devices, local(): sender_all = lax.all_gather(sender_diff, 'head', axis=1, tiled=True)  13.7 us
    dot_general x1, matrix products, local(): jnp.dot(lax.all_gather(w_out1, 'head', axis=0, tiled=True), scaled, prefe...  9.17 us
  transfers between devices with their start and end apart: 5, of which 4 were waited for; matrix products, arithmetic and copies ran while one was open for 7% of the time, Pallas kernels for 0%

commit v1 on v0

--- a/solution.py
+++ b/solution.py
@@ -2,6 +2,7 @@
 import jax.numpy as jnp
 from jax import lax
 from jax.sharding import PartitionSpec as P
+from jax.lax import all_to_all, axis_size
 
 HEAD_SIZE = 128
 epsilon = 1e-05
@@ -53,7 +54,9 @@
     ).astype(jnp.bfloat16)
     values = jnp.dot(
         normed,
-        lax.all_gather(w_value, "seq", axis=0, tiled=True),
+        jnp.concatenate(
+            all_to_all(jnp.stack([w_value for _ in range(axis_size("seq"))]), "seq", 0, 0), 0
+        ),
         preferred_element_type=jnp.float32,
     ).astype(jnp.bfloat16)
     sender_all = lax.all_gather(sender_diff, "head", axis=1, tiled=True)

time: 448 us -> 395 us (0.88)
  waiting for transfers between devices: 220 us -> 153 us
  starting transfers between devices: 0.15 us -> 13 us
    all_gather x1 -> x0, waiting for transfers between devices: 74.5 us -> none  [local(): lax.all_gather(w_value, 'seq', axis=0, tiled=True)]
    all_to_all x0 -> x1, starting transfers between devices: none -> 12.9 us  [local(): all_to_all(jnp.stack([w_value for _ in range(axis_size('seq'))]), 'seq',...]
    all_gather x1, waiting for transfers between devices: 52.5 us -> 61 us  [local(): lax.all_gather(w_out1, 'head', axis=0, tiled=True)]
  transfers between devices with their start and end apart: 5 -> 5, of which waited for: 4 -> 3; matrix products, arithmetic and copies ran while one was open for 7% -> 8% of each run, Pallas kernels for 0% -> 0%
where the time goes in v1:
time: 395 us
  blocking collectives  179 us (45%)
  waiting for transfers between devices  153 us (39%)
  matrix products  29 us (7%)
  between operations  13.2 us (3%)
  starting transfers between devices  13 us (3%)
  local copies, waits for them, and re-layouts  5.3 us (1%)
    psum x1, blocking collectives, local(): virtual = lax.psum(partial_virtual, 'seq').astype(jnp.bfloat16)  179 us
    all_gather x1, waiting for transfers between devices, local(): lax.all_gather(w_key, 'seq', axis=0, tiled=True)  76.1 us
    all_gather x1, waiting for transfers between devices, local(): lax.all_gather(w_out1, 'head', axis=0, tiled=True)  61 us
    all_to_all x1, starting transfers between devices, local(): all_to_all(jnp.stack([w_value for _ in range(axis_size('seq'))]), 'seq',...  12.9 us
    all_gather x1, waiting for transfers between devices, local(): sender_all = lax.all_gather(sender_diff, 'head', axis=1, tiled=True)  12.8 us
    dot_general x1, matrix products, local(): jnp.dot(lax.all_gather(w_out1, 'head', axis=0, tiled=True), scaled, prefe...  9.2 us
  transfers between devices with their start and end apart: 5, of which 3 were waited for; matrix products, arithmetic and copies ran while one was open for 8% of the time, Pallas kernels for 0%

profile of v1, /device:TPU:1, one launch (start us, length us, event | category | flops | bytes accessed | tf_op | source)
XLA Modules:
  0.0 395.0 jit_solution(7619253311402323624)
XLA Ops:
  6.5 0.0 copy-start
  6.5 0.7 all-gather.9.cloned.1.call-update
  7.3 0.0 all-gather.7.cloned.1.call-start
  7.3 0.7 all-gather.7.cloned.1.call-update
  8.0 0.0 all-gather.11.cloned.1.call-start
  8.1 0.7 all-gather.11.cloned.1.call-update
  8.7 2.6 stack.2
  11.4 12.9 %all-to-all-start = ((bf16[32,256,128]{2,1,0:T(8,128)(2,1)}), bf16[32,256,128]{2,1,0:T(8,128)(2,1)S(1)}, u32[]{:S(2)}, u32[]{:S(2)}) async-start(bf16[32,256,128]{2,1,0:T(8,128)(2,1)} %stack.2), calls=%async_computation | async-start | bytes 4194304 | tf_op jit(solution)/shard_map/all_to_all | solution.py:58
  24.3 0.0 all-gather.5.cloned.1.call-start
  24.3 0.5 all-gather.5.cloned.1.call-update
  24.9 0.1 constant_dynamic-slice_fusion
  24.9 0.1 copy.22
  25.0 3.1 fusion
  28.1 0.0 copy-done.3
  28.2 0.1 fusion.30
  28.3 0.0 copy-done.4
  28.3 0.1 dynamic_slice.6
  28.4 61.0 %all-gather.9.cloned.1.call-done = bf16[4096,256]{1,0:T(8,128)(2,1)} async-done(((bf16[512,256]{1,0:T(8,128)(2,1)}), bf16[4096,256]{1,0:T(8,128)(2,1)}) %all-gather.9.cloned.1.call-update) | async-done | bytes 2097168 | tf_op jit(solution)/shard_map/all_gather | solution.py:67
  89.4 1.1 mul.77
  90.5 0.0 copy-done.2
  90.5 0.4 copy-done.1
  91.0 9.2 %bitcast_multiply_fusion = f32[4096,512]{0,1:T(8,128)} fusion(f32[64,8,32,128]{3,2,1,0:T(8,128)S(1)} %bitcast.55, bf16[4096,256]{1,0:T(8,128)(2,1)S(1)} %copy-done.1, bf16[256,512]{1,0:T(8,128)(2,1)S(1)} %copy-done.2, f32[256]{0:T(256)S(1)} %dynamic_slice.6), kind=kOutput, calls=%fused_computation.5 | convolution fusion | flops 1076232192 | bytes 19137536 | tf_op jit(solution)/shard_map/dot_general | solution.py:66
  100.2 178.5 %all-reduce.1 = bf16[4096,512]{0,1:T(8,128)(2,1)} all-reduce(f32[4096,512]{0,1:T(8,128)} %bitcast_multiply_fusion), channel_id=1, replica_groups=mesh['seq'=32,'head'=8] {'seq'}, use_global_device_ids=true, to_apply=%region_1.0 | all-reduce | flops 2097152 | bytes 12582912 | tf_op jit(solution)/shard_map/psum | solution.py:75
  278.7 7.1 %fusion.31 = f32[256,512]{1,0:T(8,128)S(1)} fusion(bf16[8192,512]{1,0:T(8,128)(2,1)} %all-gather.7.cloned.1.call-done, bf16[256,8192]{1,0:T(8,128)(2,1)} %param.9, f32[8192]{0:T(1024)S(1)} %copy-done.4, f32[256]{0:T(256)S(1)} %add_rsqrt_fusion), kind=kOutput, calls=%fused_computation.34 | convolution fusion | flops 2155872256 | bytes 13140992 | tf_op jit(solution)/shard_map/dot_general | solution.py:47
  285.8 12.8 %all-gather.11.cloned.1.call-done = bf16[256,4096]{1,0:T(8,128)(2,1)} async-done(((bf16[256,512]{1,0:T(8,128)(2,1)}), bf16[256,4096]{1,0:T(8,128)(2,1)}) %all-gather.11.cloned.1.call-update) | async-done | bytes 2097168 | tf_op jit(solution)/shard_map/all_gather | solution.py:62
  298.7 4.1 %fusion.19 = bf16[32,4,8,128]{3,2,1,0:T(8,128)(2,1)S(1)} fusion(f32[256,512]{1,0:T(8,128)S(1)} %fusion.31, bf16[256,4096]{1,0:T(8,128)(2,1)} %all-gather.11.cloned.1.call-done, bf16[4096,512]{0,1:T(8,128)(2,1)} %all-reduce.1, f32[256]{0:T(256)S(1)} %add_rsqrt_fusion), kind=kOutput, calls=%fused_computation.16 | convolution fusion | flops 1074135040 | bytes 7078912 | tf_op jit(solution)/shard_map/dot_general | solution.py:76
  302.8 76.1 %all-gather.5.cloned.1.call-done = bf16[8192,128]{1,0:T(8,128)(2,1)} async-done(((bf16[256,128]{1,0:T(8,128)(2,1)}), bf16[8192,128]{1,0:T(8,128)(2,1)}) %all-gather.5.cloned.1.call-update) | async-done | bytes 2097168 | tf_op jit(solution)/shard_map/all_gather | solution.py:53
  378.9 4.5 %fusion.37 = (f32[4,256]{1,0:T(4,128)S(1)}, f32[1,4,256,256]{2,3,1,0:T(8,128)S(1)}) fusion(bf16[32,4,8,128]{3,2,1,0:T(8,128)(2,1)S(1)} %fusion.19, bf16[8192,128]{1,0:T(8,128)(2,1)} %all-gather.5.cloned.1.call-done, bf16[256,8192]{1,0:T(8,128)(2,1)} %param.9, f32[8192]{0:T(1024)S(1)} %copy-done.4, f32[256]{0:T(256)S(1)} %add_rsqrt_fusion, ...), kind=kOutput, calls=%fused_computation.35 | convolution fusion | flops 613186560 | bytes 7705600 | tf_op jit(solution)/shard_map/pehm,qem->ehpq/dot_general | solution.py:17
  383.5 0.2 fusion.24
  383.6 0.0 all-to-all-done
  383.6 4.0 %convolution_convert_fusion = bf16[128,4,256]{2,0,1:T(8,128)(2,1)S(1)} fusion(bf16[8192,128]{1,0:T(8,128)(2,1)S(1)} %bitcast.56, f32[1,4,256,256]{2,3,1,0:T(8,128)S(1)} %get-tuple-element.6, f32[4,256]{1,0:T(4,128)S(1)} %fusion.24, f32[4,256]{1,0:T(4,128)S(1)} %get-tuple-element.5, bf16[256,8192]{1,0:T(8,128)(2,1)} %param.9, f32[8192]{0:T(1024)S(1)} %copy-done.4, ...), kind=kOutput, calls=%fused_computation.14 | convolution fusion | flops 613318656 | bytes 7644160 | tf_op jit(solution)/shard_map/uczp,puv->zucv/dot_general | solution.py:28
  387.6 0.8 copy.19
  (9 shorter events, 0.0 us)
Async XLA Ops:
  6.5 18.3 %copy-start = (s32[32,32]{1,0:T(8,128)S(1)}, s32[32,32]{1,0:T(8,128)}, u32[]{:S(2)}) copy-start(s32[32,32]{1,0:T(8,128)} %param.16) | copy-start | bytes 12292
  6.5 82.9 %all-gather.9.cloned.1.call-start = ((), (), s32[]{:S(2)}) async-start(), calls=%async_computation.3 | async-start | bytes 2359296 | tf_op jit(solution)/shard_map/all_gather | solution.py:67
  7.3 271.5 %all-gather.7.cloned.1.call-start = ((), (), s32[]{:S(2)}) async-start(), calls=%async_computation.2 | async-start | bytes 8650752 | tf_op jit(solution)/shard_map/all_gather | solution.py:49
  8.0 290.6 %all-gather.11.cloned.1.call-start = ((), (), s32[]{:S(2)}) async-start(), calls=%async_computation.4 | async-start | bytes 2359296 | tf_op jit(solution)/shard_map/all_gather | solution.py:62
  11.4 16.8 %copy-start.3 = (s32[1,256]{1,0:T(1,128)S(1)}, s32[1,256]{1,0:T(1,128)}, u32[]{:S(2)}) copy-start(s32[1,256]{1,0:T(1,128)} %param.17) | copy-start | bytes 3076
  11.4 16.9 %copy-start.4 = (f32[8192]{0:T(1024)S(1)}, f32[8192]{0:T(1024)}, u32[]{:S(2)}) copy-start(f32[8192]{0:T(1024)} %param.10) | copy-start | bytes 98308
  11.4 372.2 %all-to-all-start = ((bf16[32,256,128]{2,1,0:T(8,128)(2,1)}), bf16[32,256,128]{2,1,0:T(8,128)(2,1)S(1)}, u32[]{:S(2)}, u32[]{:S(2)}) async-start(bf16[32,256,128]{2,1,0:T(8,128)(2,1)} %stack.2), calls=%async_computation | async-start | bytes 4194304 | tf_op jit(solution)/shard_map/all_to_all | solution.py:58
  24.3 354.7 %all-gather.5.cloned.1.call-start = ((), (), s32[]{:S(2)}) async-start(), calls=%async_computation.1 | async-start | bytes 2162688 | tf_op jit(solution)/shard_map/all_gather | solution.py:53
  28.4 62.2 %copy-start.2 = (bf16[256,512]{1,0:T(8,128)(2,1)S(1)}, bf16[256,512]{1,0:T(8,128)(2,1)}, u32[]{:S(2)}) copy-start(bf16[256,512]{1,0:T(8,128)(2,1)} %param.13) | copy-start | bytes 786436
  89.4 1.6 copy-start.1
Sparse Core Ops, SparseCore 0:
  9.1 80.2 all-gather.8
  92.2 133.8 all-gather.6
  227.9 70.7 all-gather.10
  301.3 77.6 all-gather.4
